TPU v7x, 256 devices: a whole 4x4x8 slice. The times are simulated.
256 devices in a mesh: rep: 2 (over z_hi), fsdp: 32 (over y, x, core), tp: 4 (over z_lo).
Axes of the slice: x: 4, y: 4, z: 8 (z_hi: 2, z_lo: 4; z = z_hi * 4 + z_lo), core: 2. Of those that a mesh axis runs over, the one named last changes fastest.
Arguments:
- delta_out: float32 [2, 8, 1792, 1792], P('rep', None, 'tp', 'fsdp'), may hold values from -6 to 6
- delta_down: float32 [2, 8, 4864, 1792], P('rep', None, 'tp', 'fsdp'), may hold values from -6 to 6
- basis: float32 [1792, 64], replicated, may hold values from -0.125 to 0.125
- anchor_out: float32 [8, 4, 448, 1792], P('rep', 'tp', 'fsdp'), may hold values from -6 to 6
- anchor_down: float32 [8, 4, 1216, 1792], P('rep', 'tp', 'fsdp'), may hold values from -6 to 6
- moment_out: float32 [8, 4, 448, 1792], P('rep', 'tp', 'fsdp'), may hold values from -3 to 3
- moment_down: float32 [8, 4, 1216, 1792], P('rep', 'tp', 'fsdp'), may hold values from -3 to 3
Outputs:
- weights_out: bfloat16 [8, 1792, 1792], P(None, 'tp', 'fsdp')
- weights_down: bfloat16 [8, 4864, 1792], P(None, 'tp', 'fsdp')
- anchor_out_new: float32 [8, 4, 448, 1792], P('rep', 'tp', 'fsdp')
- anchor_down_new: float32 [8, 4, 1216, 1792], P('rep', 'tp', 'fsdp')
- moment_out_new: float32 [8, 4, 448, 1792], P('rep', 'tp', 'fsdp')
- moment_down_new: float32 [8, 4, 1216, 1792], P('rep', 'tp', 'fsdp')
All inputs are finite; a program needn't handle non-finite values.
Results may differ from a plain program's by a relative error of at most 0.0055.
Values may be sent and summed in bfloat16 or wider, within the bound.
A program may use at most 64 MiB of HBM per device.

v0:
```python
import jax
import jax.numpy as jnp
from jax import lax
from jax.sharding import PartitionSpec as P

outer_rate = 0.7
nesterov_decay = 0.9


def owner_update(summed, basis, anchor, moment, groups):
    coef = summed / groups
    grad = jnp.einsum("lik,jk->lij", coef, basis, precision=lax.Precision.HIGHEST)
    previous = anchor[:, 0]
    velocity = moment[:, 0]
    moment_new = nesterov_decay * velocity + grad
    anchor_new = previous - outer_rate * (grad + nesterov_decay * moment_new)
    return (anchor_new, moment_new)


def per_device(delta_out, delta_down, basis, anchor_out, anchor_down, moment_out, moment_down):
    groups = lax.axis_size("rep")
    piece_cols = delta_out.shape[3]
    shard_index = lax.axis_index("fsdp")
    basis_rows = lax.dynamic_slice_in_dim(basis, shard_index * piece_cols, piece_cols, 0)
    partial_out = jnp.einsum(
        "lij,jk->lik", delta_out[0], basis_rows, precision=lax.Precision.HIGHEST
    )
    partial_down = jnp.einsum(
        "lij,jk->lik", delta_down[0], basis_rows, precision=lax.Precision.HIGHEST
    )
    layer_sums = (
        lax.psum_scatter(
            partial_out.astype(jnp.bfloat16), "rep", scatter_dimension=0, tiled=True
        ).astype(jnp.float32),
        lax.psum_scatter(
            partial_down.astype(jnp.bfloat16), "rep", scatter_dimension=0, tiled=True
        ).astype(jnp.float32),
    )
    summed_out, summed_down = (
        lax.psum_scatter(
            layer_sums[0].astype(jnp.bfloat16), "fsdp", scatter_dimension=1, tiled=True
        ).astype(jnp.float32),
        lax.psum_scatter(
            layer_sums[1].astype(jnp.bfloat16), "fsdp", scatter_dimension=1, tiled=True
        ).astype(jnp.float32),
    )
    anchor_out_new, moment_out_new = owner_update(summed_out, basis, anchor_out, moment_out, groups)
    anchor_down_new, moment_down_new = owner_update(
        summed_down, basis, anchor_down, moment_down, groups
    )
    rounded_out = anchor_out_new.astype(jnp.bfloat16)
    rounded_down = anchor_down_new.astype(jnp.bfloat16)
    placed_out, placed_down = (
        lax.all_to_all(rounded_out, "fsdp", split_axis=2, concat_axis=1, tiled=True),
        lax.all_to_all(rounded_down, "fsdp", split_axis=2, concat_axis=1, tiled=True),
    )
    weights_out, weights_down = (
        lax.all_gather(placed_out, "rep", axis=0, tiled=True),
        lax.all_gather(placed_down, "rep", axis=0, tiled=True),
    )
    return (
        weights_out,
        weights_down,
        anchor_out_new[:, None],
        anchor_down_new[:, None],
        moment_out_new[:, None],
        moment_down_new[:, None],
    )


def solution(mesh):
    return jax.shard_map(
        per_device,
        mesh=mesh,
        in_specs=(
            P("rep", None, "tp", "fsdp"),
            P("rep", None, "tp", "fsdp"),
            P(),
            P("rep", "tp", "fsdp", None),
            P("rep", "tp", "fsdp", None),
            P("rep", "tp", "fsdp", None),
            P("rep", "tp", "fsdp", None),
        ),
        out_specs=(
            P(None, "tp", "fsdp"),
            P(None, "tp", "fsdp"),
            P("rep", "tp", "fsdp", None),
            P("rep", "tp", "fsdp", None),
            P("rep", "tp", "fsdp", None),
            P("rep", "tp", "fsdp", None),
        ),
        check_vma=False,
    )
```

profile of v0, /device:TPU:37, one launch (start us, length us, event | category | flops | bytes accessed | tf_op | source)
XLA Modules:
  0.0 313.3 jit_solution(11942777162929042482)
XLA Ops:
  7.2 0.0 copy-start
  7.2 0.0 reduce-scatter.3.cloned.1.call-start
  7.2 3.2 %fusion.2 = bf16[8,448,64]{1,2,0:T(8,128)(2,1)} fusion(f32[1,8,448,56]{2,3,1,0:T(8,128)} %param.7, f32[1792,64]{0,1:T(8,128)} %param.9, s32[]{:T(128)S(6)} %select_n.3), kind=kOutput, calls=%fused_computation.5 | convolution fusion | flops 154370048 | bytes 1409028 | tf_op jit(solution)/shard_map/lij,jk->lik/dot_general | solution.py:25
  10.4 0.0 reduce-scatter.3.cloned.1.call-update
  10.4 0.0 reduce-scatter.5.cloned.1.call-start
  10.5 0.0 copy-done
  10.5 4.2 %fusion = bf16[8,1216,64]{1,2,0:T(8,128)(2,1)} fusion(f32[1,8,1216,56]{2,3,1,0:T(8,128)S(1)} %copy-done, f32[1792,64]{0,1:T(8,128)} %param.9, s32[]{:T(128)S(6)} %select_n.3), kind=kOutput, calls=%fused_computation.1 | convolution fusion | flops 419004416 | bytes 3457028 | tf_op jit(solution)/shard_map/lij,jk->lik/dot_general | solution.py:28
  14.7 0.0 reduce-scatter.5.cloned.1.call-update
  14.7 0.0 all-reduce.5.cloned.1.call-start
  14.8 27.7 %reduce-scatter.3.cloned.1.call-done = bf16[4,448,64]{1,2,0:T(8,128)(2,1)} async-done(((bf16[8,448,64]{1,2,0:T(8,128)(2,1)}), bf16[4,448,64]{1,2,0:T(8,128)(2,1)}) %reduce-scatter.3.cloned.1.call-update) | async-done | bytes 229392 | tf_op jit(solution)/shard_map/reduce_scatter | solution.py:32
  42.4 2.0 copy.35
  44.4 43.5 %reduce-scatter.5.cloned.1.call-done = bf16[4,1216,64]{1,2,0:T(8,128)(2,1)} async-done(((bf16[8,1216,64]{1,2,0:T(8,128)(2,1)}), bf16[4,1216,64]{1,2,0:T(8,128)(2,1)}) %reduce-scatter.5.cloned.1.call-update) | async-done | bytes 622608 | tf_op jit(solution)/shard_map/reduce_scatter | solution.py:35
  87.9 3.2 %copy.43 = bf16[4,1216,64]{2,0,1:T(4,128)(2,1)} copy(bf16[4,1216,64]{1,2,0:T(8,128)(2,1)} %reduce-scatter.5.cloned.1.call-done) | data formatting | bytes 1245184 | tf_op jit(solution)/shard_map/reduce_scatter | solution.py:35
  91.1 0.0 all-reduce.5.cloned.1.call-update
  91.1 0.0 all-gather.2.cloned.1.call-start
  91.2 0.6 copy-done.4
  91.8 0.6 dynamic-slice
  93.0 111.4 %all-reduce.5.cloned.1.call-done = (bf16[4,448,64]{2,0,1:T(4,128)(2,1)}, bf16[4,1216,64]{2,0,1:T(4,128)(2,1)}) async-done(((bf16[4,448,64]{2,0,1:T(4,128)(2,1)}, bf16[4,1216,64]{2,0,1:T(4,128)(2,1)}), (bf16[4,448,64]{2,0,1:T(4,128)(2,1)}, bf16[4,1216,64]{2,0,1:T(4,128)(2,1)})) %all-reduce.5.cloned.1.call-update) | async-done | bytes 851984
  204.4 0.8 convert_multiply_fusion
  205.2 4.2 %fusion.20 = (f32[4,1,38,1792]{3,2,0,1:T(8,128)}, bf16[4,38,1792]{2,1,0:T(8,128)(2,1)}, f32[4,1,38,1792]{3,2,0,1:T(8,128)S(1)}) fusion(f32[4,1,38,1792]{3,1,2,0:T(1,128)} %param.13, f32[4,1,38,1792]{3,1,2,0:T(1,128)} %param.11, f32[1792,64]{0,1:T(8,128)} %param.9, f32[4,38,64]{2,0,1:T(4,128)S(1)} %convert_multiply_fusion), kind=kOutput, calls=%fused_computation.32 | convolution fusion | flops 211097600 | bytes 5400576 | tf_op jit(solution)/shard_map/lik,jk->lij/dot_general | solution.py:12
  209.4 3.6 %copy.46 = bf16[4,38,1792]{1,0,2:T(4,128)(2,1)} copy(bf16[4,38,1792]{2,1,0:T(8,128)(2,1)} %get-tuple-element.27) | data formatting | bytes 1089536 | tf_op jit(solution)/shard_map/convert_element_type | solution.py:52
  212.9 5.8 %reshape.22 = bf16[32,2,4256]{2,1,0:T(2,128)(2,1)} reshape(bf16[1792,4,38]{2,1,0:T(4,128)(2,1)} %bitcast.82) | data formatting | bytes 1089536
  218.7 16.4 %all_to_all.36 = bf16[32,2,4256]{2,1,0:T(2,128)(2,1)} all-to-all(bf16[32,2,4256]{2,1,0:T(2,128)(2,1)} %reshape.22), channel_id=1, replica_groups=mesh['rep'=2,'fsdp'=32,'tp'=4] {'fsdp'}, dimensions={0} | all-to-all | bytes 1089536 | tf_op jit(solution)/shard_map/all_to_all | solution.py:55
  235.1 7.4 %reshape.23 = bf16[1792,4,38]{2,1,0:T(4,128)(2,1)} reshape(bf16[32,2,4256]{2,1,0:T(2,128)(2,1)} %all_to_all.36) | data formatting | bytes 1089536
  242.6 3.5 %copy.100 = bf16[4,38,32,56]{1,2,3,0:T(8,128)(2,1)} copy(bf16[4,38,32,56]{1,0,3,2:T(4,128)(2,1)} %bitcast.80) | data formatting | bytes 1089536 | tf_op jit(solution)/shard_map/all_to_all | solution.py:55
  246.0 4.7 %all_to_all.33 = bf16[4,1216,56]{1,2,0:T(8,128)(2,1)} reshape(bf16[4,32,38,56]{2,1,3,0:T(8,128)(2,1)} %bitcast.81) | data formatting | bytes 1089536 | tf_op jit(solution)/shard_map/all_to_all | solution.py:55
  250.7 0.0 all-gather.2.cloned.1.call-update
  251.3 0.0 copy-start.1
  251.3 1.2 copy.101
  252.5 0.7 convert_multiply_fusion.1
  253.2 0.0 copy-done.1
  253.2 2.6 fusion.18
  255.9 3.3 %copy.39 = bf16[4,14,1792]{1,0,2:T(4,128)(2,1)} copy(bf16[4,14,1792]{2,1,0:T(8,128)(2,1)} %get-tuple-element.30) | data formatting | bytes 401408 | tf_op jit(solution)/shard_map/convert_element_type | solution.py:51
  259.2 4.8 %reshape.20 = bf16[32,2,1568]{2,1,0:T(2,128)(2,1)} reshape(bf16[1792,4,14]{2,1,0:T(4,128)(2,1)} %bitcast.83) | data formatting | bytes 401408
  264.0 7.1 %all-to-all-start = ((bf16[32,2,1568]{2,1,0:T(2,128)(2,1)}), bf16[32,2,1568]{2,1,0:T(2,128)(2,1)}, u32[]{:S(2)}, u32[]{:S(2)}) async-start(bf16[32,2,1568]{2,1,0:T(2,128)(2,1)} %reshape.20), calls=%async_computation.1 | async-start | bytes 425984 | tf_op jit(solution)/shard_map/all_to_all | solution.py:54
  271.1 3.4 %copy.50 = f32[4,1,38,1792]{3,1,2,0:T(1,128)} copy(f32[4,1,38,1792]{3,2,0,1:T(8,128)} %get-tuple-element.26) | data formatting | bytes 2179072
  274.4 2.1 copy.52
  276.5 1.2 copy.49
  277.7 0.0 copy-done.2
  277.7 1.2 copy.51
  278.9 0.0 all-to-all-done
  278.9 6.8 %reshape.21 = bf16[1792,4,14]{2,1,0:T(4,128)(2,1)} reshape(bf16[32,2,1568]{2,1,0:T(2,128)(2,1)} %all-to-all-done) | data formatting | bytes 401408
  285.6 3.4 %copy.53 = bf16[4,14,32,56]{3,2,0,1:T(8,128)(2,1)S(1)} copy(bf16[4,14,32,56]{1,0,3,2:T(4,128)(2,1)} %bitcast.84) | data formatting | bytes 401408 | tf_op jit(solution)/shard_map/all_to_all | solution.py:54
  289.0 0.2 copy.41
  289.3 0.3 copy.42
  289.6 14.2 %all_gather.6 = bf16[8,448,56]{1,2,0:T(8,128)(2,1)S(1)} all-gather(bf16[4,448,56]{1,2,0:T(8,128)(2,1)S(1)} %copy.42), channel_id=1, replica_groups=mesh['rep'=2,'fsdp'=32,'tp'=4] {'rep'}, dimensions={0}, use_global_device_ids=true | all-gather | bytes 602112 | tf_op jit(solution)/shard_map/all_gather | solution.py:58
  303.7 0.8 copy.106
  304.5 2.3 copy.107
  (5 shorter events, 0.0 us)
Async XLA Ops:
  7.2 3.3 %copy-start = (f32[1,8,1216,56]{2,3,1,0:T(8,128)S(1)}, f32[1,8,1216,56]{2,3,1,0:T(8,128)}, u32[]{:S(2)}) copy-start(f32[1,8,1216,56]{2,3,1,0:T(8,128)} %param.8) | copy-start | bytes 6537220
  7.2 35.2 %reduce-scatter.3.cloned.1.call-start = ((), (), s32[]{:S(2)}) async-start(), calls=%async_computation.4 | async-start | bytes 786432 | tf_op jit(solution)/shard_map/reduce_scatter | solution.py:32
  10.4 77.4 %reduce-scatter.5.cloned.1.call-start = ((), (), s32[]{:S(2)}) async-start(), calls=%async_computation.5 | async-start | bytes 1966080 | tf_op jit(solution)/shard_map/reduce_scatter | solution.py:35
  14.7 189.7 %all-reduce.5.cloned.1.call-start = ((), (), s32[]{:S(2)}) async-start(), calls=%async_computation.7 | async-start | bytes 3407872
  91.1 0.7 copy-start.4
  91.1 212.6 %all-gather.2.cloned.1.call-start = ((), (), s32[]{:S(2)}) async-start(), calls=%async_computation.6 | async-start | bytes 1720320 | tf_op jit(solution)/shard_map/all_gather | solution.py:59
  251.3 1.9 copy-start.1
  264.0 14.9 %all-to-all-start = ((bf16[32,2,1568]{2,1,0:T(2,128)(2,1)}), bf16[32,2,1568]{2,1,0:T(2,128)(2,1)}, u32[]{:S(2)}, u32[]{:S(2)}) async-start(bf16[32,2,1568]{2,1,0:T(2,128)(2,1)} %reshape.20), calls=%async_computation.1 | async-start | bytes 425984 | tf_op jit(solution)/shard_map/all_to_all | solution.py:54
  274.4 2.1 copy-start.3
  274.4 3.3 %copy-start.2 = (f32[4,1,14,1792]{3,2,0,1:T(8,128)S(1)}, f32[4,1,14,1792]{3,2,0,1:T(8,128)}, u32[]{:S(2)}) copy-start(f32[4,1,14,1792]{3,2,0,1:T(8,128)} %get-tuple-element.31) | copy-start | bytes 1204228
Sparse Core Ops, SparseCore 0:
  11.1 31.2 reduce-scatter.2
  45.1 42.7 reduce-scatter.4
  91.9 112.5 all-reduce.4
  250.8 43.0 all-gather.1
where the time goes:
time: 318 us; the launch traced here: 313 us
  waiting for transfers between devices  183 us (58%)
  local copies, waits for them, and re-layouts  62.1 us (20%)
  blocking collectives  30.6 us (10%)
  between operations  15.2 us (5%)
  matrix products  14.1 us (4%)
  starting transfers between devices  7.27 us (2%)
    unnamed x5, waiting for transfers between devices  111 us
    reduce_scatter x1, waiting for transfers between devices, per_device(): lax.psum_scatter(partial_down.astype(jnp.bfloat16), 'rep', scatter_dimens...  43.5 us
    unnamed x22, local copies, waits for them, and re-layouts  38 us
    reduce_scatter x1, waiting for transfers between devices, per_device(): lax.psum_scatter(partial_out.astype(jnp.bfloat16), 'rep', scatter_dimensi...  27.7 us
    all_to_all x1, blocking collectives, per_device(): lax.all_to_all(rounded_down, 'fsdp', split_axis=2, concat_axis=1, tiled=T...  16.4 us
    all_gather x1, blocking collectives, per_device(): lax.all_gather(placed_out, 'rep', axis=0, tiled=True)  14.2 us
    all_to_all x2, local copies, waits for them, and re-layouts, per_device(): lax.all_to_all(rounded_down, 'fsdp', split_axis=2, concat_axis=1, tiled=T...  8.1 us
    all_to_all x1, starting transfers between devices, per_device(): lax.all_to_all(rounded_out, 'fsdp', split_axis=2, concat_axis=1, tiled=True)  7.1 us
  transfers between devices with their start and end apart: 5, of which 3 were waited for; matrix products, arithmetic and copies ran while one was open for 12% of the time, Pallas kernels for 0%

commit v1 on v0

v1 whole, which is shorter than its diff:
```python
import jax
import jax.numpy as jnp
from jax import lax
from jax.experimental import pallas as pl
from jax.experimental.pallas import tpu as pltpu
from jax.sharding import PartitionSpec as P

MESH = pl.DeviceIdType.MESH
outer_rate = 0.7
nesterov_decay = 0.9
base_decay = outer_rate * nesterov_decay * nesterov_decay
grad_gain = outer_rate * (1.0 + nesterov_decay)

LANES = 128
COLS = 56
ROWS_OUT, ROWS_DOWN = 448, 1216
OWN_OUT, OWN_DOWN = 14, 38
WIDE_OUT, WIDE_DOWN = 512, 1280
WIDE = WIDE_OUT + WIDE_DOWN
MSG = 2 * (OWN_OUT + OWN_DOWN)
CHUNKS = 14
N_FSDP = 32
CHIPS = 16
PIECE = 16
F32, BF16 = jnp.float32, jnp.bfloat16


def column_window(load_chunk, index):
    first = (7 * index) // 16
    offset = COLS * index - LANES * first
    second = jnp.minimum(first + 1, CHUNKS - 1)
    return load_chunk(first), load_chunk(second), offset


def own_basis(basis_ref, f):
    low, high, offset = column_window(
        lambda k: basis_ref[:, pl.ds(pl.multiple_of(k * LANES, LANES), LANES)], f
    )
    lane = lax.broadcasted_iota(jnp.int32, low.shape, 1)
    window = jnp.where(lane >= offset, low, high)
    window = pltpu.roll(window, lax.rem(LANES - offset, LANES), 1)
    return jnp.where(lane < COLS, window, 0.0)


def split(x):
    high = x.astype(BF16)
    return high, (x - high.astype(F32)).astype(BF16)


def exchange_kernel(
    dout_hbm, ddown_hbm, basis_hbm, aout_hbm, adown_hbm, mout_hbm, mdown_hbm,
    rows_hbm, coef_hbm,
    dout, ddown, basis, aout, adown, mout, mdown,
    stack, part, part16, cross, half, gathered, mine, theirs, final, base, src,
    in_sem, local_sem, base_send, base_recv, core_send, core_recv, rs_send, rs_recv,
    rep_send, rep_recv, ag_send, ag_recv, fw_send, fw_recv,
):
    r = lax.axis_index("rep")
    f = lax.axis_index("fsdp")
    t = lax.axis_index("tp")
    chip, core = f // 2, lax.rem(f, 2)
    other = 1 - core
    me = r * N_FSDP + f

    loads = [
        pltpu.make_async_copy(a, b, in_sem.at[i])
        for i, (a, b) in enumerate(
            ((basis_hbm, basis), (dout_hbm, dout), (ddown_hbm, ddown), (aout_hbm, aout),
             (mout_hbm, mout), (adown_hbm, adown), (mdown_hbm, mdown))
        )
    ]
    for copy in loads:
        copy.start()

    barrier = pltpu.get_barrier_semaphore()

    def greet(i, carry):
        peer = lax.rem(me + i, 2 * N_FSDP)
        pl.semaphore_signal(
            barrier, inc=1, device_id=(peer // N_FSDP, lax.rem(peer, N_FSDP), t), device_id_type=MESH
        )
        return carry

    lax.fori_loop(1, 2 * N_FSDP, greet, 0)

    stack[...] = jnp.zeros_like(stack)
    for copy in loads[:3]:
        copy.wait()
    high, low = split(own_basis(basis, f))
    high2 = high.astype(F32)
    left = jnp.concatenate([(high2 + pltpu.roll(high2, 64, 1)).astype(BF16), low], axis=1)

    def project(l, carry):
        for ref, lanes in ((dout, pl.ds(0, ROWS_OUT)), (ddown, pl.ds(WIDE_OUT, ROWS_DOWN))):
            hi, lo = split(ref[l])
            stack[0:COLS, lanes] = hi
            stack[64 : 64 + COLS, lanes] = lo
            stack[128 : 128 + COLS, lanes] = hi
        coef = jnp.dot(left, stack[...], preferred_element_type=F32)
        for a in range(2):
            for b in range(2):
                rows = coef[PIECE * (2 * a + b) : PIECE * (2 * a + b + 1)]
                part[2 * l + a, b] = rows
                part16[2 * l + a, b] = rows.astype(BF16)
        return carry

    lax.fori_loop(0, 8, project, 0)

    for copy in loads[3:]:
        copy.wait()

    def combine(c, carry):
        for h in range(2):
            for a, m, count, at in ((aout, mout, 28, 0), (adown, mdown, 76, 28)):
                rows = pl.ds(c + CHUNKS * count * h, count, stride=CHUNKS)
                base[h, c, at : at + count, :] = a[rows, :] - base_decay * m[rows, :]
        return carry

    lax.fori_loop(0, CHUNKS, combine, 0)

    def pack(j, carry):
        low0, high0, offset = column_window(lambda k: base[0, k], j)
        low1, high1, _ = column_window(lambda k: base[1, k], j)
        lane = lax.broadcasted_iota(jnp.int32, low0.shape, 1)
        first = pltpu.roll(jnp.where(lane >= offset, low0, high0), lax.rem(LANES - offset, LANES), 1)
        second = pltpu.roll(jnp.where(lane >= offset, low1, high1), lax.rem(LANES + 64 - offset, LANES), 1)
        src[j] = jnp.where(lane < 64, first, second).astype(BF16)
        return carry

    lax.fori_loop(0, N_FSDP, pack, 0)

    pl.semaphore_wait(barrier, 2 * N_FSDP - 1)

    partner_core = (r, 2 * chip + other, t)
    core_copy = pltpu.make_async_remote_copy(
        part16.at[:, other], cross, core_send, core_recv, device_id=partner_core, device_id_type=MESH
    )
    core_copy.start()

    def send_across(i, carry):
        j = lax.rem(f + i, N_FSDP)
        pltpu.make_async_remote_copy(
            src.at[j], rows_hbm.at[r, f], base_send.at[0], base_recv.at[0],
            device_id=(1 - r, j, t), device_id_type=MESH,
        ).start()
        return carry

    def send_within(i, carry):
        j = lax.rem(f + i, N_FSDP)
        pltpu.make_async_remote_copy(
            src.at[j], rows_hbm.at[r, f], base_send.at[1], base_recv.at[1],
            device_id=(r, j, t), device_id_type=MESH,
        ).start()
        return carry

    lax.fori_loop(0, 16, send_across, 0)
    own_rows = pltpu.make_async_copy(src.at[f], rows_hbm.at[r, f], local_sem.at[0])
    own_rows.start()

    core_copy.wait_recv()

    def halve(p, carry):
        half[p] = (part[p, core] + cross[p].astype(F32)).astype(BF16)
        return carry

    lax.fori_loop(0, CHIPS, halve, 0)
    gathered[chip] = half[chip]

    def send_half(i, carry):
        p = lax.rem(chip + i, CHIPS)
        pltpu.make_async_remote_copy(
            half.at[p], gathered.at[chip], rs_send, rs_recv,
            device_id=(r, 2 * p + core, t), device_id_type=MESH,
        ).start()
        return carry

    lax.fori_loop(1, CHIPS, send_half, 0)
    lax.fori_loop(1, N_FSDP, send_within, 0)

    rs_wait = pltpu.make_async_remote_copy(
        half.at[pl.ds(0, CHIPS - 1)], gathered.at[pl.ds(0, CHIPS - 1)], rs_send, rs_recv,
        device_id=partner_core, device_id_type=MESH,
    )
    rs_wait.wait_recv()
    total = gathered[0].astype(F32)
    for p in range(1, CHIPS):
        total = total + gathered[p].astype(F32)
    mine[...] = total.astype(BF16)
    rep_copy = pltpu.make_async_remote_copy(
        mine, theirs, rep_send, rep_recv, device_id=(1 - r, f, t), device_id_type=MESH
    )
    rep_copy.start()
    lax.fori_loop(16, N_FSDP, send_across, 0)
    rep_copy.wait_recv()
    final[...] = (0.5 * (mine[...].astype(F32) + theirs[...].astype(F32))).astype(BF16)

    def send_final(i, carry):
        p = lax.rem(chip + i, CHIPS)
        pltpu.make_async_remote_copy(
            final, coef_hbm.at[chip, core], ag_send, ag_recv.at[chip],
            device_id=(r, 2 * p + core, t), device_id_type=MESH,
        ).start()
        return carry

    pltpu.make_async_remote_copy(
        final, coef_hbm.at[chip, core], ag_send, fw_recv, device_id=partner_core, device_id_type=MESH
    ).start()
    lax.fori_loop(1, CHIPS, send_final, 0)
    own_coef = pltpu.make_async_copy(final, coef_hbm.at[chip, core], local_sem.at[1])
    own_coef.start()

    def forward(i, carry):
        p = lax.rem(chip + CHIPS - i, CHIPS)
        pltpu.make_async_remote_copy(
            final, coef_hbm.at[p, core], ag_send, ag_recv.at[p], device_id=partner_core, device_id_type=MESH
        ).wait_recv()
        pltpu.make_async_remote_copy(
            coef_hbm.at[p, core], coef_hbm.at[p, core], fw_send, fw_recv,
            device_id=partner_core, device_id_type=MESH,
        ).start()
        return carry

    lax.fori_loop(1, CHIPS, forward, 0)

    own_rows.wait()
    own_coef.wait()
    core_copy.wait_send()
    rs_wait.wait_send()
    rep_copy.wait_send()

    def settle(sent, landed, send, recv):
        copy = pltpu.make_async_remote_copy(
            sent, landed, send, recv, device_id=partner_core, device_id_type=MESH
        )
        copy.wait_send()
        copy.wait_recv()

    settle(src, rows_hbm.at[1 - r], base_send.at[0], base_recv.at[0])
    most = pl.ds(0, N_FSDP - 1)
    settle(src.at[most], rows_hbm.at[r, most], base_send.at[1], base_recv.at[1])
    pltpu.make_async_remote_copy(
        half, half, ag_send, fw_recv, device_id=partner_core, device_id_type=MESH
    ).wait_send()
    pltpu.make_async_remote_copy(
        half.at[pl.ds(0, CHIPS - 1)], half.at[pl.ds(0, CHIPS - 1)], fw_send, fw_recv,
        device_id=partner_core, device_id_type=MESH,
    ).wait_send()
    pltpu.make_async_remote_copy(
        half, coef_hbm.at[:, other], fw_send, fw_recv, device_id=partner_core, device_id_type=MESH
    ).wait_recv()


def exchange(dout, ddown, basis, aout, adown, mout, mdown):
    any_spec = pl.BlockSpec(memory_space=pl.ANY)
    sem = pltpu.SemaphoreType.DMA
    return pl.pallas_call(
        exchange_kernel,
        name="exchange",
        out_shape=(
            jax.ShapeDtypeStruct((2, N_FSDP, MSG, LANES), BF16),
            jax.ShapeDtypeStruct((CHIPS, 2, PIECE, WIDE), BF16),
        ),
        in_specs=[any_spec] * 7,
        out_specs=(any_spec, any_spec),
        scratch_shapes=[
            pltpu.VMEM(dout.shape, F32),
            pltpu.VMEM(ddown.shape, F32),
            pltpu.VMEM(basis.shape, F32),
            pltpu.VMEM(aout.shape, F32),
            pltpu.VMEM(adown.shape, F32),
            pltpu.VMEM(mout.shape, F32),
            pltpu.VMEM(mdown.shape, F32),
            pltpu.VMEM((256, WIDE), BF16),
            pltpu.VMEM((CHIPS, 2, PIECE, WIDE), F32),
            pltpu.VMEM((CHIPS, 2, PIECE, WIDE), BF16),
            pltpu.VMEM((CHIPS, PIECE, WIDE), BF16),
            pltpu.VMEM((CHIPS, PIECE, WIDE), BF16),
            pltpu.VMEM((CHIPS, PIECE, WIDE), BF16),
            pltpu.VMEM((PIECE, WIDE), BF16),
            pltpu.VMEM((PIECE, WIDE), BF16),
            pltpu.VMEM((PIECE, WIDE), BF16),
            pltpu.VMEM((2, CHUNKS, MSG, LANES), F32),
            pltpu.VMEM((N_FSDP, MSG, LANES), BF16),
            sem((7,)), sem((2,)), sem((2,)), sem((2,)), sem, sem, sem, sem,
            sem, sem, sem, sem((CHIPS,)), sem, sem,
        ],
        compiler_params=pltpu.CompilerParams(
            collective_id=0, has_side_effects=True, vmem_limit_bytes=56 * 1024 * 1024
        ),
    )(dout, ddown, basis, aout, adown, mout, mdown)


TN = (((0,), (0,)), ((), ()))
NT = (((1,), (1,)), ((), ()))


def placement(first, count, height, shift, own, tile):
    shape = (count, height, 2 * LANES)
    source = lax.broadcasted_iota(jnp.int32, shape, 0) + first
    lane = lax.broadcasted_iota(jnp.int32, shape, 2)
    second = lane >= LANES
    row = jnp.where(second, lane - LANES, lane) + LANES * tile
    at = lax.broadcasted_iota(jnp.int32, shape, 1) - shift - jnp.where(second, own, 0)
    hit = (row - own * source == at) & (at >= 0) & (at < own)
    return jnp.where(hit, 1.0, 0.0).astype(BF16).reshape(count * height, 2 * LANES)


def finish_kernel(
    place, rows, coef, basis, aout, adown, mout, mdown,
    wout, wdown, aout_new, adown_new, mout_new, mdown_new, grad,
):
    r, f = place[0], place[1]
    high, low = split(own_basis(basis, f))
    left = jnp.concatenate([high, low], axis=0)

    def project(l, carry):
        c = coef[l]
        g = lax.dot_general(left, jnp.concatenate([c, c], axis=0), TN, preferred_element_type=F32)
        grad[l] = grad_gain * g[:COLS]
        return carry

    lax.fori_loop(0, 8, project, 0)

    for out, own, count, height, begin, shift, total, lane0 in (
        (wout, OWN_OUT, 10, 32, 0, 0, ROWS_OUT, 0),
        (wdown, OWN_DOWN, 5, 80, 24, 4, ROWS_DOWN, WIDE_OUT),
    ):
        for tile in range((total + LANES - 1) // LANES):
            first = min((LANES * tile) // own, N_FSDP - count)
            pick = placement(first, count, height, shift, own, tile)
            width = min(LANES, total - LANES * tile)
            for g in range(2):
                got = rows[g, first : first + count, begin : begin + height, :].reshape(count * height, LANES)
                placed = lax.dot_general(got, pick, TN, preferred_element_type=F32)
                for h in range(2):
                    for b in range(2):
                        l = 4 * g + 2 * h + b
                        lanes = pl.ds(lane0 + LANES * tile, width)
                        value = placed[64 * h : 64 * h + COLS, LANES * b : LANES * b + width] - grad[l, :, lanes]
                        out[l, :, pl.ds(LANES * tile, width)] = value.astype(BF16)

    bhigh, blow = split(basis[...])
    for a, m, a_new, m_new, own, lane0, wide in (
        (aout, mout, aout_new, mout_new, OWN_OUT, 0, WIDE_OUT),
        (adown, mdown, adown_new, mdown_new, OWN_DOWN, WIDE_OUT, WIDE_DOWN),
    ):
        n = 4 * own
        picked = jnp.zeros((n, 64), F32)
        for l in range(4):
            row = lax.broadcasted_iota(jnp.int32, (n, wide), 0) - own * l
            lane = lax.broadcasted_iota(jnp.int32, (n, wide), 1)
            hit = (lane - own * f == row) & (row >= 0) & (row < own)
            one = jnp.where(hit, 1.0, 0.0).astype(BF16)
            picked = picked + lax.dot_general(
                one, coef[4 * r + l, :, pl.ds(lane0, wide)], NT, preferred_element_type=F32
            )
        picked = picked.astype(BF16)
        step = jnp.dot(picked, bhigh, preferred_element_type=F32) + jnp.dot(
            picked, blow, preferred_element_type=F32
        )
        for c in range(CHUNKS):
            at = pl.ds(c, n, stride=CHUNKS)
            g = step[:, LANES * c : LANES * (c + 1)]
            moment = nesterov_decay * m[at, :] + g
            m_new[at, :] = moment
            a_new[at, :] = a[at, :] - outer_rate * (g + nesterov_decay * moment)


def finish(place, rows, coef, basis, aout, adown, mout, mdown):
    vmem = pl.BlockSpec(memory_space=pltpu.VMEM)
    return pl.pallas_call(
        finish_kernel,
        name="finish",
        out_shape=(
            jax.ShapeDtypeStruct((8, COLS, ROWS_OUT), BF16),
            jax.ShapeDtypeStruct((8, COLS, ROWS_DOWN), BF16),
            jax.ShapeDtypeStruct(aout.shape, F32),
            jax.ShapeDtypeStruct(adown.shape, F32),
            jax.ShapeDtypeStruct(aout.shape, F32),
            jax.ShapeDtypeStruct(adown.shape, F32),
        ),
        in_specs=[pl.BlockSpec(memory_space=pltpu.SMEM)] + [vmem] * 7,
        out_specs=(vmem,) * 6,
        scratch_shapes=[pltpu.VMEM((8, COLS, WIDE), F32)],
        compiler_params=pltpu.CompilerParams(vmem_limit_bytes=56 * 1024 * 1024),
    )(place, rows, coef, basis, aout, adown, mout, mdown)


def per_device(delta_out, delta_down, basis, anchor_out, anchor_down, moment_out, moment_down):
    dout = jnp.transpose(delta_out[0], (0, 2, 1))
    ddown = jnp.transpose(delta_down[0], (0, 2, 1))
    basis_t = basis.T
    flat = [x.reshape(-1, LANES) for x in (anchor_out, anchor_down, moment_out, moment_down)]
    rows, coef = exchange(dout, ddown, basis_t, *flat)
    place = jnp.stack([lax.axis_index("rep"), lax.axis_index("fsdp")]).astype(jnp.int32)
    wout, wdown, aout, adown, mout, mdown = finish(
        place, rows, coef.reshape(8, 64, WIDE), basis_t, *flat
    )
    return (
        jnp.transpose(wout, (0, 2, 1)),
        jnp.transpose(wdown, (0, 2, 1)),
        aout.reshape(anchor_out.shape),
        adown.reshape(anchor_down.shape),
        mout.reshape(moment_out.shape),
        mdown.reshape(moment_down.shape),
    )


def solution(mesh):
    return jax.shard_map(
        per_device,
        mesh=mesh,
        in_specs=(
            P("rep", None, "tp", "fsdp"),
            P("rep", None, "tp", "fsdp"),
            P(),
            P("rep", "tp", "fsdp", None),
            P("rep", "tp", "fsdp", None),
            P("rep", "tp", "fsdp", None),
            P("rep", "tp", "fsdp", None),
        ),
        out_specs=(
            P(None, "tp", "fsdp"),
            P(None, "tp", "fsdp"),
            P("rep", "tp", "fsdp", None),
            P("rep", "tp", "fsdp", None),
            P("rep", "tp", "fsdp", None),
            P("rep", "tp", "fsdp", None),
        ),
        check_vma=False,
    )
```

time: 318 us -> 87.3 us (0.27)
  the two profiles are of different devices: /device:TPU:37 before, /device:TPU:47 now
where the time goes in v1:
time: 87.3 us
  Pallas kernels  86.1 us (99%)
    pallas_call x1, Pallas kernels, exchange(): pl.pallas_call(exchange_kernel, name='exchange', out_shape=(jax.ShapeDtyp...  76.1 us
    pallas_call x1, Pallas kernels, finish(): pl.pallas_call(finish_kernel, name='finish', out_shape=(jax.ShapeDtypeStr...  9.95 us

profile of v1, /device:TPU:47, one launch (start us, length us, event | category | flops | bytes accessed | tf_op | source)
XLA Modules:
  0.0 87.3 jit_solution(9071648713873073090)
XLA Ops:
  0.6 0.6 pad_add_fusion.place
  1.2 76.1 %exchange.1 = (bf16[2,32,104,128]{3,2,1,0:T(8,128)(2,1)}, bf16[16,2,16,1792]{3,2,1,0:T(8,128)(2,1)}) custom-call(f32[8,56,448]{2,1,0:T(8,128)} %bitcast.32, f32[8,56,1216]{2,1,0:T(8,128)} %bitcast.24, f32[64,1792]{1,0:T(8,128)} %bitcast.25, f32[784,128]{1,0:T(8,128)} %bitcast.28, f32[2128,128]{1,0:T(8,128)} %bitcast.20, f32[784,128]{1,0:T(8,128)} %bitcast.30, ...), custom_call_target="tpu_custom_call" | custom-call | tf_op jit(solution)/shard_map/exchange/pallas_call | solution.py:256
  77.3 9.9 %finish.1 = (bf16[8,56,448]{2,1,0:T(8,128)(2,1)}, bf16[8,56,1216]{2,1,0:T(8,128)(2,1)}, f32[784,128]{1,0:T(8,128)}, f32[2128,128]{1,0:T(8,128)}, f32[784,128]{1,0:T(8,128)}, /*index=5*/f32[2128,128]{1,0:T(8,128)}) custom-call(s32[2]{0:T(128)} %pad_add_fusion.place, bf16[2,32,104,128]{3,2,1,0:T(8,128)(2,1)} %get-tuple-element.14.rows, ...), custom_call_target="tpu_custom_call" | custom-call | tf_op jit(solution)/shard_map/finish/pallas_call | solution.py:371

commit v2 on v1

--- a/solution.py
+++ b/solution.py
@@ -22,6 +22,7 @@
 N_FSDP = 32
 CHIPS = 16
 PIECE = 16
+FIRST = 16
 F32, BF16 = jnp.float32, jnp.bfloat16
 
 
@@ -52,7 +53,7 @@
     rows_hbm, coef_hbm,
     dout, ddown, basis, aout, adown, mout, mdown,
     stack, part, part16, cross, half, gathered, mine, theirs, final, base, src,
-    in_sem, local_sem, base_send, base_recv, core_send, core_recv, rs_send, rs_recv,
+    in_sem, local_sem, base_send, base_recv, across_send, across_recv, core_send, core_recv, rs_send, rs_recv,
     rep_send, rep_recv, ag_send, ag_recv, fw_send, fw_recv,
 ):
     r = lax.axis_index("rep")
@@ -60,13 +61,12 @@
     t = lax.axis_index("tp")
     chip, core = f // 2, lax.rem(f, 2)
     other = 1 - core
-    me = r * N_FSDP + f
 
     loads = [
         pltpu.make_async_copy(a, b, in_sem.at[i])
         for i, (a, b) in enumerate(
-            ((basis_hbm, basis), (dout_hbm, dout), (ddown_hbm, ddown), (aout_hbm, aout),
-             (mout_hbm, mout), (adown_hbm, adown), (mdown_hbm, mdown))
+            ((aout_hbm, aout), (mout_hbm, mout), (adown_hbm, adown), (mdown_hbm, mdown),
+             (basis_hbm, basis), (dout_hbm, dout), (ddown_hbm, ddown))
         )
     ]
     for copy in loads:
@@ -75,16 +75,69 @@
     barrier = pltpu.get_barrier_semaphore()
 
     def greet(i, carry):
-        peer = lax.rem(me + i, 2 * N_FSDP)
         pl.semaphore_signal(
-            barrier, inc=1, device_id=(peer // N_FSDP, lax.rem(peer, N_FSDP), t), device_id_type=MESH
+            barrier, inc=1, device_id=(r, lax.rem(f + i, N_FSDP), t), device_id_type=MESH
         )
         return carry
 
-    lax.fori_loop(1, 2 * N_FSDP, greet, 0)
+    lax.fori_loop(1, N_FSDP, greet, 0)
+    pl.semaphore_signal(barrier, inc=1, device_id=(1 - r, f, t), device_id_type=MESH)
+
+    for copy in loads[:4]:
+        copy.wait()
+
+    def combine(c, carry):
+        for h in range(2):
+            for a, m, count, at in ((aout, mout, 28, 0), (adown, mdown, 76, 28)):
+                rows = pl.ds(c + CHUNKS * count * h, count, stride=CHUNKS)
+                base[h, c, at : at + count, :] = a[rows, :] - base_decay * m[rows, :]
+        return carry
+
+    lax.fori_loop(0, CHUNKS, combine, 0)
+
+    def pack(j, carry):
+        low0, high0, offset = column_window(lambda k: base[0, k], j)
+        low1, high1, _ = column_window(lambda k: base[1, k], j)
+        lane = lax.broadcasted_iota(jnp.int32, low0.shape, 1)
+        first = pltpu.roll(jnp.where(lane >= offset, low0, high0), lax.rem(LANES - offset, LANES), 1)
+        second = pltpu.roll(jnp.where(lane >= offset, low1, high1), lax.rem(LANES + 64 - offset, LANES), 1)
+        src[j] = jnp.where(lane < 64, first, second).astype(BF16)
+        return carry
+
+    lax.fori_loop(0, N_FSDP, pack, 0)
+
+    pl.semaphore_wait(barrier, N_FSDP)
+
+    def send_within(i, carry):
+        j = lax.rem(f + i, N_FSDP)
+        pltpu.make_async_remote_copy(
+            src.at[j], rows_hbm.at[r, f], base_send, base_recv.at[f],
+            device_id=(r, j, t), device_id_type=MESH,
+        ).start()
+        return carry
+
+    def send_across(i, carry):
+        p = lax.rem(f + N_FSDP - i, N_FSDP)
+        pltpu.make_async_remote_copy(
+            src.at[p], rows_hbm.at[r, p], base_send, base_recv.at[p],
+            device_id=(1 - r, f, t), device_id_type=MESH,
+        ).wait_recv()
+        pltpu.make_async_remote_copy(
+            rows_hbm.at[r, p], rows_hbm.at[r, p], across_send, across_recv,
+            device_id=(1 - r, f, t), device_id_type=MESH,
+        ).start()
+        return carry
+
+    lax.fori_loop(1, FIRST, send_within, 0)
+    pltpu.make_async_remote_copy(
+        src.at[f], rows_hbm.at[r, f], across_send, across_recv,
+        device_id=(1 - r, f, t), device_id_type=MESH,
+    ).start()
+    own_rows = pltpu.make_async_copy(src.at[f], rows_hbm.at[r, f], local_sem.at[0])
+    own_rows.start()
 
     stack[...] = jnp.zeros_like(stack)
-    for copy in loads[:3]:
+    for copy in loads[4:]:
         copy.wait()
     high, low = split(own_basis(basis, f))
     high2 = high.astype(F32)
@@ -106,57 +159,11 @@
 
     lax.fori_loop(0, 8, project, 0)
 
-    for copy in loads[3:]:
-        copy.wait()
-
-    def combine(c, carry):
-        for h in range(2):
-            for a, m, count, at in ((aout, mout, 28, 0), (adown, mdown, 76, 28)):
-                rows = pl.ds(c + CHUNKS * count * h, count, stride=CHUNKS)
-                base[h, c, at : at + count, :] = a[rows, :] - base_decay * m[rows, :]
-        return carry
-
-    lax.fori_loop(0, CHUNKS, combine, 0)
-
-    def pack(j, carry):
-        low0, high0, offset = column_window(lambda k: base[0, k], j)
-        low1, high1, _ = column_window(lambda k: base[1, k], j)
-        lane = lax.broadcasted_iota(jnp.int32, low0.shape, 1)
-        first = pltpu.roll(jnp.where(lane >= offset, low0, high0), lax.rem(LANES - offset, LANES), 1)
-        second = pltpu.roll(jnp.where(lane >= offset, low1, high1), lax.rem(LANES + 64 - offset, LANES), 1)
-        src[j] = jnp.where(lane < 64, first, second).astype(BF16)
-        return carry
-
-    lax.fori_loop(0, N_FSDP, pack, 0)
-
-    pl.semaphore_wait(barrier, 2 * N_FSDP - 1)
-
     partner_core = (r, 2 * chip + other, t)
     core_copy = pltpu.make_async_remote_copy(
         part16.at[:, other], cross, core_send, core_recv, device_id=partner_core, device_id_type=MESH
     )
     core_copy.start()
-
-    def send_across(i, carry):
-        j = lax.rem(f + i, N_FSDP)
-        pltpu.make_async_remote_copy(
-            src.at[j], rows_hbm.at[r, f], base_send.at[0], base_recv.at[0],
-            device_id=(1 - r, j, t), device_id_type=MESH,
-        ).start()
-        return carry
-
-    def send_within(i, carry):
-        j = lax.rem(f + i, N_FSDP)
-        pltpu.make_async_remote_copy(
-            src.at[j], rows_hbm.at[r, f], base_send.at[1], base_recv.at[1],
-            device_id=(r, j, t), device_id_type=MESH,
-        ).start()
-        return carry
-
-    lax.fori_loop(0, 16, send_across, 0)
-    own_rows = pltpu.make_async_copy(src.at[f], rows_hbm.at[r, f], local_sem.at[0])
-    own_rows.start()
-
     core_copy.wait_recv()
 
     def halve(p, carry):
@@ -175,7 +182,8 @@
         return carry
 
     lax.fori_loop(1, CHIPS, send_half, 0)
-    lax.fori_loop(1, N_FSDP, send_within, 0)
+    lax.fori_loop(FIRST, N_FSDP, send_within, 0)
+    lax.fori_loop(1, FIRST, send_across, 0)
 
     rs_wait = pltpu.make_async_remote_copy(
         half.at[pl.ds(0, CHIPS - 1)], gathered.at[pl.ds(0, CHIPS - 1)], rs_send, rs_recv,
@@ -190,7 +198,6 @@
         mine, theirs, rep_send, rep_recv, device_id=(1 - r, f, t), device_id_type=MESH
     )
     rep_copy.start()
-    lax.fori_loop(16, N_FSDP, send_across, 0)
     rep_copy.wait_recv()
     final[...] = (0.5 * (mine[...].astype(F32) + theirs[...].astype(F32))).astype(BF16)
 
@@ -208,6 +215,7 @@
     lax.fori_loop(1, CHIPS, send_final, 0)
     own_coef = pltpu.make_async_copy(final, coef_hbm.at[chip, core], local_sem.at[1])
     own_coef.start()
+    lax.fori_loop(FIRST, N_FSDP, send_across, 0)
 
     def forward(i, carry):
         p = lax.rem(chip + CHIPS - i, CHIPS)
@@ -228,16 +236,15 @@
     rs_wait.wait_send()
     rep_copy.wait_send()
 
-    def settle(sent, landed, send, recv):
-        copy = pltpu.make_async_remote_copy(
-            sent, landed, send, recv, device_id=partner_core, device_id_type=MESH
-        )
-        copy.wait_send()
-        copy.wait_recv()
-
-    settle(src, rows_hbm.at[1 - r], base_send.at[0], base_recv.at[0])
     most = pl.ds(0, N_FSDP - 1)
-    settle(src.at[most], rows_hbm.at[r, most], base_send.at[1], base_recv.at[1])
+    pltpu.make_async_remote_copy(
+        src.at[most], src.at[most], base_send, across_recv, device_id=partner_core, device_id_type=MESH
+    ).wait_send()
+    across = pltpu.make_async_remote_copy(
+        src, rows_hbm.at[1 - r], across_send, across_recv, device_id=partner_core, device_id_type=MESH
+    )
+    across.wait_send()
+    across.wait_recv()
     pltpu.make_async_remote_copy(
         half, half, ag_send, fw_recv, device_id=partner_core, device_id_type=MESH
     ).wait_send()
@@ -281,7 +288,7 @@
             pltpu.VMEM((PIECE, WIDE), BF16),
             pltpu.VMEM((2, CHUNKS, MSG, LANES), F32),
             pltpu.VMEM((N_FSDP, MSG, LANES), BF16),
-            sem((7,)), sem((2,)), sem((2,)), sem((2,)), sem, sem, sem, sem,
+            sem((7,)), sem((2,)), sem, sem((N_FSDP,)), sem, sem, sem, sem, sem, sem,
             sem, sem, sem, sem((CHIPS,)), sem, sem,
         ],
         compiler_params=pltpu.CompilerParams(

time: 87.3 us -> 76.6 us (0.88)
  the two profiles are of different devices: /device:TPU:47 before, /device:TPU:37 now
where the time goes in v2:
time: 76.6 us
  Pallas kernels  75.4 us (98%)
    pallas_call x1, Pallas kernels, exchange(): pl.pallas_call(exchange_kernel, name='exchange', out_shape=(jax.ShapeDtyp...  65.4 us
    pallas_call x1, Pallas kernels, finish(): pl.pallas_call(finish_kernel, name='finish', out_shape=(jax.ShapeDtypeStr...  9.94 us

profile of v2, /device:TPU:37, one launch (start us, length us, event | category | flops | bytes accessed | tf_op | source)
XLA Modules:
  0.0 76.6 jit_solution(1413017287948096750)
XLA Ops:
  0.6 0.6 pad_add_fusion.place
  1.2 65.4 %exchange.1 = (bf16[2,32,104,128]{3,2,1,0:T(8,128)(2,1)}, bf16[16,2,16,1792]{3,2,1,0:T(8,128)(2,1)}) custom-call(f32[8,56,448]{2,1,0:T(8,128)} %bitcast.32, f32[8,56,1216]{2,1,0:T(8,128)} %bitcast.24, f32[64,1792]{1,0:T(8,128)} %bitcast.25, f32[784,128]{1,0:T(8,128)} %bitcast.28, f32[2128,128]{1,0:T(8,128)} %bitcast.20, f32[784,128]{1,0:T(8,128)} %bitcast.30, ...), custom_call_target="tpu_custom_call" | custom-call | tf_op jit(solution)/shard_map/exchange/pallas_call | solution.py:263
  66.6 9.9 %finish.1 = (bf16[8,56,448]{2,1,0:T(8,128)(2,1)}, bf16[8,56,1216]{2,1,0:T(8,128)(2,1)}, f32[784,128]{1,0:T(8,128)}, f32[2128,128]{1,0:T(8,128)}, f32[784,128]{1,0:T(8,128)}, /*index=5*/f32[2128,128]{1,0:T(8,128)}) custom-call(s32[2]{0:T(128)} %pad_add_fusion.place, bf16[2,32,104,128]{3,2,1,0:T(8,128)(2,1)} %get-tuple-element.14.rows, ...), custom_call_target="tpu_custom_call" | custom-call | tf_op jit(solution)/shard_map/finish/pallas_call | solution.py:378

commit v3 on v2

--- a/solution.py
+++ b/solution.py
@@ -201,34 +201,62 @@
     rep_copy.wait_recv()
     final[...] = (0.5 * (mine[...].astype(F32) + theirs[...].astype(F32))).astype(BF16)
 
-    def send_final(i, carry):
-        p = lax.rem(chip + i, CHIPS)
-        pltpu.make_async_remote_copy(
-            final, coef_hbm.at[chip, core], ag_send, ag_recv.at[chip],
-            device_id=(r, 2 * p + core, t), device_id_type=MESH,
+    x, y = lax.rem(chip, 4), chip // 4
+    stride_u, stride_v = 1 + 3 * core, 4 - 3 * core
+    u = (1 - core) * x + core * y
+    v = (1 - core) * y + core * x
+
+    def chip_at(du, dv):
+        return lax.rem(u + du, 4) * stride_u + lax.rem(v + dv, 4) * stride_v
+
+    def send_coef(source, s, target):
+        pltpu.make_async_remote_copy(
+            source, coef_hbm.at[s, core], ag_send, ag_recv.at[s],
+            device_id=(r, 2 * target + core, t), device_id_type=MESH,
         ).start()
-        return carry
-
+
+    def send_final_u(i, carry):
+        send_coef(final, chip, chip_at(i, 0))
+        return carry
+
+    def send_final_v(i, carry):
+        send_coef(final, chip, chip_at(0, i))
+        return carry
+
+    def forward(s):
+        pltpu.make_async_remote_copy(
+            final, coef_hbm.at[s, core], ag_send, ag_recv.at[s], device_id=partner_core, device_id_type=MESH
+        ).wait_recv()
+        pltpu.make_async_remote_copy(
+            coef_hbm.at[s, core], coef_hbm.at[s, core], fw_send, fw_recv,
+            device_id=partner_core, device_id_type=MESH,
+        ).start()
+
+    def relay(k, carry):
+        s = chip_at(4 - k, 0)
+        forward(s)
+
+        def send(i, inner):
+            send_coef(coef_hbm.at[s, core], s, chip_at(0, i))
+            return inner
+
+        return lax.fori_loop(1, 4, send, carry)
+
+    def collect(i, carry):
+        forward(chip_at(i // 3, 1 + lax.rem(i, 3)))
+        return carry
+
+    lax.fori_loop(1, 4, send_final_u, 0)
     pltpu.make_async_remote_copy(
         final, coef_hbm.at[chip, core], ag_send, fw_recv, device_id=partner_core, device_id_type=MESH
     ).start()
-    lax.fori_loop(1, CHIPS, send_final, 0)
+    lax.fori_loop(1, 4, send_final_v, 0)
     own_coef = pltpu.make_async_copy(final, coef_hbm.at[chip, core], local_sem.at[1])
     own_coef.start()
-    lax.fori_loop(FIRST, N_FSDP, send_across, 0)
-
-    def forward(i, carry):
-        p = lax.rem(chip + CHIPS - i, CHIPS)
-        pltpu.make_async_remote_copy(
-            final, coef_hbm.at[p, core], ag_send, ag_recv.at[p], device_id=partner_core, device_id_type=MESH
-        ).wait_recv()
-        pltpu.make_async_remote_copy(
-            coef_hbm.at[p, core], coef_hbm.at[p, core], fw_send, fw_recv,
-            device_id=partner_core, device_id_type=MESH,
-        ).start()
-        return carry
-
-    lax.fori_loop(1, CHIPS, forward, 0)
+    lax.fori_loop(FIRST, 24, send_across, 0)
+    lax.fori_loop(1, 4, relay, 0)
+    lax.fori_loop(24, N_FSDP, send_across, 0)
+    lax.fori_loop(0, 12, collect, 0)
 
     own_rows.wait()
     own_coef.wait()

time: 76.6 us -> 74.3 us (0.970)
  Pallas kernels: 75.4 us -> 72.5 us
    pallas_call x1, Pallas kernels: 65.4 us -> 62.5 us  [exchange(): pl.pallas_call(exchange_kernel, name='exchange', out_shape=(jax.ShapeDtyp...]
where the time goes in v3:
time: 74.3 us; the launch traced here: 73.6 us
  Pallas kernels  72.5 us (98%)
    pallas_call x1, Pallas kernels, exchange(): pl.pallas_call(exchange_kernel, name='exchange', out_shape=(jax.ShapeDtyp...  62.5 us
    pallas_call x1, Pallas kernels, finish(): pl.pallas_call(finish_kernel, name='finish', out_shape=(jax.ShapeDtypeStr...  9.94 us

profile of v3, /device:TPU:37, one launch (start us, length us, event | category | flops | bytes accessed | tf_op | source)
XLA Modules:
  0.0 73.6 jit_solution(7615945888923674687)
XLA Ops:
  0.6 0.6 pad_add_fusion.place
  1.2 62.5 %exchange.1 = (bf16[2,32,104,128]{3,2,1,0:T(8,128)(2,1)}, bf16[16,2,16,1792]{3,2,1,0:T(8,128)(2,1)}) custom-call(f32[8,56,448]{2,1,0:T(8,128)} %bitcast.32, f32[8,56,1216]{2,1,0:T(8,128)} %bitcast.24, f32[64,1792]{1,0:T(8,128)} %bitcast.25, f32[784,128]{1,0:T(8,128)} %bitcast.28, f32[2128,128]{1,0:T(8,128)} %bitcast.20, f32[784,128]{1,0:T(8,128)} %bitcast.30, ...), custom_call_target="tpu_custom_call" | custom-call | tf_op jit(solution)/shard_map/exchange/pallas_call | solution.py:291
  63.7 9.9 %finish.1 = (bf16[8,56,448]{2,1,0:T(8,128)(2,1)}, bf16[8,56,1216]{2,1,0:T(8,128)(2,1)}, f32[784,128]{1,0:T(8,128)}, f32[2128,128]{1,0:T(8,128)}, f32[784,128]{1,0:T(8,128)}, /*index=5*/f32[2128,128]{1,0:T(8,128)}) custom-call(s32[2]{0:T(128)} %pad_add_fusion.place, bf16[2,32,104,128]{3,2,1,0:T(8,128)(2,1)} %get-tuple-element.14.rows, ...), custom_call_target="tpu_custom_call" | custom-call | tf_op jit(solution)/shard_map/finish/pallas_call | solution.py:406

commit v4 on v3

--- a/solution.py
+++ b/solution.py
@@ -52,9 +52,9 @@
     dout_hbm, ddown_hbm, basis_hbm, aout_hbm, adown_hbm, mout_hbm, mdown_hbm,
     rows_hbm, coef_hbm,
     dout, ddown, basis, aout, adown, mout, mdown,
-    stack, part, part16, cross, half, gathered, mine, theirs, final, base, src,
+    stack, part, part16, cross, half, gathered, line, landed, mine, theirs, final, base, src,
     in_sem, local_sem, base_send, base_recv, across_send, across_recv, core_send, core_recv, rs_send, rs_recv,
-    rep_send, rep_recv, ag_send, ag_recv, fw_send, fw_recv,
+    rep_send, rep_recv, ag_send, ag_recv, fw_send, fw_recv, line_send, line_recv,
 ):
     r = lax.axis_index("rep")
     f = lax.axis_index("fsdp")
@@ -171,36 +171,6 @@
         return carry
 
     lax.fori_loop(0, CHIPS, halve, 0)
-    gathered[chip] = half[chip]
-
-    def send_half(i, carry):
-        p = lax.rem(chip + i, CHIPS)
-        pltpu.make_async_remote_copy(
-            half.at[p], gathered.at[chip], rs_send, rs_recv,
-            device_id=(r, 2 * p + core, t), device_id_type=MESH,
-        ).start()
-        return carry
-
-    lax.fori_loop(1, CHIPS, send_half, 0)
-    lax.fori_loop(FIRST, N_FSDP, send_within, 0)
-    lax.fori_loop(1, FIRST, send_across, 0)
-
-    rs_wait = pltpu.make_async_remote_copy(
-        half.at[pl.ds(0, CHIPS - 1)], gathered.at[pl.ds(0, CHIPS - 1)], rs_send, rs_recv,
-        device_id=partner_core, device_id_type=MESH,
-    )
-    rs_wait.wait_recv()
-    total = gathered[0].astype(F32)
-    for p in range(1, CHIPS):
-        total = total + gathered[p].astype(F32)
-    mine[...] = total.astype(BF16)
-    rep_copy = pltpu.make_async_remote_copy(
-        mine, theirs, rep_send, rep_recv, device_id=(1 - r, f, t), device_id_type=MESH
-    )
-    rep_copy.start()
-    rep_copy.wait_recv()
-    final[...] = (0.5 * (mine[...].astype(F32) + theirs[...].astype(F32))).astype(BF16)
-
     x, y = lax.rem(chip, 4), chip // 4
     stride_u, stride_v = 1 + 3 * core, 4 - 3 * core
     u = (1 - core) * x + core * y
@@ -208,6 +178,57 @@
 
     def chip_at(du, dv):
         return lax.rem(u + du, 4) * stride_u + lax.rem(v + dv, 4) * stride_v
+
+    for w in range(4):
+        gathered[4 * u + w] = half[u * stride_u + w * stride_v]
+
+    def send_half(i, carry):
+        du, w = 1 + i // 4, lax.rem(i, 4)
+        pltpu.make_async_remote_copy(
+            half.at[lax.rem(u + du, 4) * stride_u + w * stride_v], gathered.at[4 * u + w], rs_send, rs_recv,
+            device_id=(r, 2 * chip_at(du, 0) + core, t), device_id_type=MESH,
+        ).start()
+        return carry
+
+    lax.fori_loop(0, 12, send_half, 0)
+    lax.fori_loop(1, FIRST, send_across, 0)
+
+    rs_wait = pltpu.make_async_remote_copy(
+        half.at[pl.ds(0, 12)], gathered.at[pl.ds(0, 12)], rs_send, rs_recv,
+        device_id=partner_core, device_id_type=MESH,
+    )
+    rs_wait.wait_recv()
+    for w in range(4):
+        total = gathered[w].astype(F32)
+        for p in range(1, 4):
+            total = total + gathered[4 * p + w].astype(F32)
+        line[w] = total.astype(BF16)
+    landed[v] = line[v]
+
+    def send_line(i, carry):
+        pltpu.make_async_remote_copy(
+            line.at[lax.rem(v + i, 4)], landed.at[v], line_send, line_recv,
+            device_id=(r, 2 * chip_at(0, i) + core, t), device_id_type=MESH,
+        ).start()
+        return carry
+
+    lax.fori_loop(1, 4, send_line, 0)
+    lax.fori_loop(FIRST, N_FSDP, send_within, 0)
+    line_wait = pltpu.make_async_remote_copy(
+        line.at[pl.ds(0, 3)], landed.at[pl.ds(0, 3)], line_send, line_recv,
+        device_id=partner_core, device_id_type=MESH,
+    )
+    line_wait.wait_recv()
+    total = landed[0].astype(F32)
+    for p in range(1, 4):
+        total = total + landed[p].astype(F32)
+    mine[...] = total.astype(BF16)
+    rep_copy = pltpu.make_async_remote_copy(
+        mine, theirs, rep_send, rep_recv, device_id=(1 - r, f, t), device_id_type=MESH
+    )
+    rep_copy.start()
+    rep_copy.wait_recv()
+    final[...] = (0.5 * (mine[...].astype(F32) + theirs[...].astype(F32))).astype(BF16)
 
     def send_coef(source, s, target):
         pltpu.make_async_remote_copy(
@@ -262,6 +283,7 @@
     own_coef.wait()
     core_copy.wait_send()
     rs_wait.wait_send()
+    line_wait.wait_send()
     rep_copy.wait_send()
 
     most = pl.ds(0, N_FSDP - 1)
@@ -311,13 +333,15 @@
             pltpu.VMEM((CHIPS, PIECE, WIDE), BF16),
             pltpu.VMEM((CHIPS, PIECE, WIDE), BF16),
             pltpu.VMEM((CHIPS, PIECE, WIDE), BF16),
+            pltpu.VMEM((4, PIECE, WIDE), BF16),
+            pltpu.VMEM((4, PIECE, WIDE), BF16),
             pltpu.VMEM((PIECE, WIDE), BF16),
             pltpu.VMEM((PIECE, WIDE), BF16),
             pltpu.VMEM((PIECE, WIDE), BF16),
             pltpu.VMEM((2, CHUNKS, MSG, LANES), F32),
             pltpu.VMEM((N_FSDP, MSG, LANES), BF16),
             sem((7,)), sem((2,)), sem, sem((N_FSDP,)), sem, sem, sem, sem, sem, sem,
-            sem, sem, sem, sem((CHIPS,)), sem, sem,
+            sem, sem, sem, sem((CHIPS,)), sem, sem, sem, sem,
         ],
         compiler_params=pltpu.CompilerParams(
             collective_id=0, has_side_effects=True, vmem_limit_bytes=56 * 1024 * 1024

time: 74.3 us -> 69.8 us (0.939)
  Pallas kernels: 72.5 us -> 67.4 us
    pallas_call x1, Pallas kernels: 62.5 us -> 57.5 us  [exchange(): pl.pallas_call(exchange_kernel, name='exchange', out_shape=(jax.ShapeDtyp...]
where the time goes in v4:
time: 69.8 us; the launch traced here: 68.6 us
  Pallas kernels  67.4 us (97%)
    pallas_call x1, Pallas kernels, exchange(): pl.pallas_call(exchange_kernel, name='exchange', out_shape=(jax.ShapeDtyp...  57.5 us
    pallas_call x1, Pallas kernels, finish(): pl.pallas_call(finish_kernel, name='finish', out_shape=(jax.ShapeDtypeStr...  9.94 us

profile of v4, /device:TPU:37, one launch (start us, length us, event | category | flops | bytes accessed | tf_op | source)
XLA Modules:
  0.0 68.6 jit_solution(4765173731471293040)
XLA Ops:
  0.6 0.6 pad_add_fusion.place
  1.2 57.5 %exchange.1 = (bf16[2,32,104,128]{3,2,1,0:T(8,128)(2,1)}, bf16[16,2,16,1792]{3,2,1,0:T(8,128)(2,1)}) custom-call(f32[8,56,448]{2,1,0:T(8,128)} %bitcast.32, f32[8,56,1216]{2,1,0:T(8,128)} %bitcast.24, f32[64,1792]{1,0:T(8,128)} %bitcast.25, f32[784,128]{1,0:T(8,128)} %bitcast.28, f32[2128,128]{1,0:T(8,128)} %bitcast.20, f32[784,128]{1,0:T(8,128)} %bitcast.30, ...), custom_call_target="tpu_custom_call" | custom-call | tf_op jit(solution)/shard_map/exchange/pallas_call | solution.py:313
  58.7 9.9 %finish.1 = (bf16[8,56,448]{2,1,0:T(8,128)(2,1)}, bf16[8,56,1216]{2,1,0:T(8,128)(2,1)}, f32[784,128]{1,0:T(8,128)}, f32[2128,128]{1,0:T(8,128)}, f32[784,128]{1,0:T(8,128)}, /*index=5*/f32[2128,128]{1,0:T(8,128)}) custom-call(s32[2]{0:T(128)} %pad_add_fusion.place, bf16[2,32,104,128]{3,2,1,0:T(8,128)(2,1)} %get-tuple-element.14.rows, ...), custom_call_target="tpu_custom_call" | custom-call | tf_op jit(solution)/shard_map/finish/pallas_call | solution.py:430
